TPU v7x, 32 devices: a whole 2x2x4 slice. The times are simulated.
32 devices in a mesh: expert: 16 (over z, x, core), tensor: 2 (over y).
Axes of the slice: x: 2, y: 2, z: 4, core: 2. Of those that a mesh axis runs over, the one named last changes fastest.
Arguments:
- query: bfloat16 [128, 8192], P(('expert', 'tensor')), may hold values from -6 to 6
- cache_keys: bfloat16 [128, 128, 4, 128], P(('expert', 'tensor')), may hold values from -6 to 6
- cache_values: bfloat16 [128, 128, 4, 128], P(('expert', 'tensor')), may hold values from -6 to 6
- lengths: int32 [128], P(('expert', 'tensor')), may hold values from 2 to 128, as said below
- residual: bfloat16 [128, 4096], P('tensor', 'expert'), may hold values from -12 to 12
- out_proj: bfloat16 [4096, 8192], P('expert', 'tensor'), may hold values from -0.0625 to 0.0625
- norm_gain: bfloat16 [4096], P('expert'), may hold values from 0.099609375 to 1.8984375
- expert_ids: int32 [128, 8], replicated, may hold values from 0 to 15, all different within a row; in each aligned block of 128 rows (0 to 127, 128 to 255, ...) at most 128 rows name the same one
- gate_scores: bfloat16 [128, 8], replicated, may hold values from 0.019897461 to 1
- w_gate: bfloat16 [16, 1536, 4096], P('expert', 'tensor'), may hold values from -0.09375 to 0.09375
- w_up: bfloat16 [16, 1536, 4096], P('expert', 'tensor'), may hold values from -0.09375 to 0.09375
- w_down: bfloat16 [16, 1536, 4096], P('expert', 'tensor'), may hold values from -0.15625 to 0.15625
Outputs:
- attn_residual: bfloat16 [128, 4096], P('tensor', 'expert')
- expert_mix: bfloat16 [128, 4096], P('tensor', 'expert')
Inputs may be any that keep to these rules, and one draw needn't show every extreme that they name: `expert_ids`: each row names 8 different experts; no expert is named by more than 128 rows, and one by exactly 128. `lengths`: some row has exactly 128.
All inputs are finite; a program needn't handle non-finite values.
Results may differ from a plain program's by a relative error of at most 0.018.
Values may be sent and summed in bfloat16 or wider, within the bound.
A program may use at most 64 MiB of HBM per device.

v0:
```python
import jax
import jax.numpy as jnp
from jax import lax
from jax.sharding import PartitionSpec as P

CAP = 128


floor_value = -1e30
epsilon = 1e-06


def softmax_parts(queries, key_block, value_block, usable, score_scale):
    scores = (
        jnp.einsum("rkgd,rpkd->rkgp", queries, key_block, preferred_element_type=jnp.float32)
        * score_scale
    )
    usable_mask = usable[:, None, None, :]
    peak = jnp.max(jnp.where(usable_mask, scores, floor_value), axis=-1)
    raw_weights = jnp.where(usable_mask, jnp.exp(scores - peak[..., None]), 0.0)
    weight_sum = jnp.sum(raw_weights, axis=-1)
    weighted = jnp.einsum("rkgp,rpkd->rkgd", raw_weights, value_block.astype(jnp.float32))
    return (weight_sum, weighted)


def body(
    query,
    cache_keys,
    cache_values,
    lengths,
    residual,
    out_proj,
    norm_gain,
    expert_ids,
    gate_scores,
    w_gate,
    w_up,
    w_down,
):
    row_count, full_heads_width = query.shape
    cache_len = cache_keys.shape[1]
    kv_count = cache_keys.shape[2]
    head_size = cache_keys.shape[3]
    head_count = full_heads_width // head_size
    group_size = head_count // kv_count
    score_scale = head_size ** (-0.5)
    usable = jnp.arange(cache_len, dtype=jnp.int32)[None, :] < lengths[:, None]
    grouped = query.reshape(row_count, kv_count, group_size, head_size)
    weight_sum, weighted = softmax_parts(grouped, cache_keys, cache_values, usable, score_scale)
    context_rows_own = (
        (weighted / weight_sum[..., None]).astype(jnp.bfloat16).reshape(row_count, full_heads_width)
    )
    context = lax.all_to_all(context_rows_own, "tensor", split_axis=1, concat_axis=0, tiled=True)
    attn_part = jnp.dot(
        lax.all_gather(context, "expert", axis=0, tiled=True),
        out_proj.T,
        preferred_element_type=jnp.float32,
    )
    attn_share = lax.psum_scatter(attn_part, "tensor", scatter_dimension=0, tiled=True)
    hidden_state = residual.astype(jnp.float32) + attn_share
    squares = lax.psum(jnp.sum(hidden_state * hidden_state, axis=1), "expert")
    full_width = hidden_state.shape[1] * lax.axis_size("expert")
    normed_share = (
        hidden_state
        * lax.rsqrt(squares[:, None] / full_width + epsilon)
        * norm_gain.astype(jnp.float32)[None, :]
    ).astype(jnp.bfloat16)
    normed = lax.all_gather(normed_share, "tensor", axis=0, tiled=True)
    experts_local = w_gate.shape[0]
    expert_count = experts_local * lax.axis_size("expert")
    rows_all, choose_count = expert_ids.shape
    flat_ids = expert_ids.reshape(-1)
    onehot = (flat_ids[:, None] == jnp.arange(expert_count, dtype=jnp.int32)[None, :]).astype(
        jnp.int32
    )
    slot_index = jnp.sum((jnp.cumsum(onehot, axis=0) - onehot) * onehot, axis=1)
    destination = flat_ids * CAP + slot_index
    source = jnp.arange(rows_all * choose_count, dtype=jnp.int32) // choose_count
    slot_owner = (
        jnp.full((expert_count * CAP,), -1, jnp.int32)
        .at[destination]
        .set(source)
        .reshape(expert_count, CAP)
    )
    gate_weight = gate_scores.astype(jnp.float32)
    gate_weight = gate_weight / jnp.sum(gate_weight, axis=1, keepdims=True)
    filled = slot_owner >= 0
    outgoing = jnp.where(
        filled[..., None], normed[jnp.maximum(slot_owner, 0)], jnp.zeros((), jnp.bfloat16)
    )
    arrived = lax.all_to_all(outgoing, "expert", split_axis=0, concat_axis=2, tiled=True)
    gate_proj = jnp.einsum("ecd,efd->ecf", arrived, w_gate, preferred_element_type=jnp.float32)
    up_proj = jnp.einsum("ecd,efd->ecf", arrived, w_up, preferred_element_type=jnp.float32)
    activation = (jax.nn.silu(gate_proj) * up_proj).astype(jnp.bfloat16)
    result = jnp.einsum("ecf,efd->ecd", activation, w_down, preferred_element_type=jnp.float32)
    returned = lax.all_to_all(
        result.astype(jnp.bfloat16), "expert", split_axis=2, concat_axis=0, tiled=True
    ).astype(result.dtype)
    result_table = returned.reshape(expert_count * CAP, returned.shape[2])
    gathered = result_table[destination]
    mixed_rows = jnp.sum(
        gathered.reshape(rows_all, choose_count, -1) * gate_weight[:, :, None], axis=1
    )
    mixed_share = lax.psum_scatter(
        mixed_rows.astype(jnp.bfloat16), "tensor", scatter_dimension=0, tiled=True
    )
    return (hidden_state.astype(jnp.bfloat16), mixed_share)


def solution(mesh):
    in_specs = (
        P(("expert", "tensor"), None),
        P(("expert", "tensor"), None, None, None),
        P(("expert", "tensor"), None, None, None),
        P(("expert", "tensor")),
        P("tensor", "expert"),
        P("expert", "tensor"),
        P("expert"),
        P(),
        P(),
        P("expert", "tensor", None),
        P("expert", "tensor", None),
        P("expert", "tensor", None),
    )
    out_specs = (P("tensor", "expert"), P("tensor", "expert"))
    return jax.shard_map(body, mesh=mesh, in_specs=in_specs, out_specs=out_specs, check_vma=False)
```

profile of v0, /device:TPU:0, one launch (start us, length us, event | category | flops | bytes accessed | tf_op | source)
XLA Modules:
  0.0 259.9 jit_solution(9676230513321024557)
XLA Ops:
  7.2 0.9 iota_compare_fusion.2
  8.1 0.8 copy.43
  9.0 1.5 select_reduce_fusion
  10.5 2.5 fusion
  13.0 1.4 fusion.19
  14.4 0.1 copy.33
  14.4 8.2 %all_to_all.43 = bf16[4,2,4096]{2,0,1:T(4,128)(2,1)S(1)} all-to-all(bf16[4,2,4096]{2,0,1:T(4,128)(2,1)S(1)} %copy.33), channel_id=1, replica_groups=mesh['expert'=16,'tensor'=2] {'tensor'}, dimensions={1} | all-to-all | bytes 131072 | tf_op jit(solution)/shard_map/all_to_all | solution.py:53
  22.6 0.6 all_to_all.35
  23.3 0.0 reduce-scatter.3.cloned.1.call-start
  23.3 0.8 copy.35
  24.1 0.1 eq.29
  24.2 0.1 eq.25
  24.3 0.7 broadcast_multiply_fusion
  25.0 0.1 copy.34
  25.1 0.1 mul.65
  25.2 4.5 %reduce-window.6 = s32[16,8,128]{2,1,0:T(8,128)S(1)} reduce-window(s32[16,8,128]{2,1,0:T(8,128)S(1)} %fusion.39, s32[]{:T(128)} %constant.41.clone.1), window={size=1x1x128 pad=0_0x0_0x127_0}, to_apply=%region_3.4 | reduce-window | flops 2080768 | bytes 131076 | tf_op jit(solution)/shard_map/reduce-window
  29.7 0.1 slice.12
  29.8 0.1 copy.37
  30.0 0.1 copy.38
  30.1 0.1 broadcast_add_fusion
  30.2 4.3 %scatter_custom_fusion = s32[2048]{0:T(1024)S(1)} fusion(s32[1024]{0:T(1024)S(1)} %bitcast.83, s32[1024]{0:T(1024)S(1)} %add_select_fusion, s32[]{:T(128)} %constant.39.clone.1), kind=kCustom, calls=%fused_computation.60 | custom fusion | bytes 8196 | tf_op jit(solution)/shard_map/scatter | solution.py:82
  34.5 27.2 %all-gather.2.cloned.1.call-done = bf16[128,4096]{1,0:T(8,128)(2,1)} async-done(((bf16[8,4096]{1,0:T(8,128)(2,1)}), bf16[128,4096]{1,0:T(8,128)(2,1)}) %all-gather.2.cloned.1.call-update) | async-done | bytes 1048592 | tf_op jit(solution)/shard_map/all_gather | solution.py:55
  61.7 2.7 %fusion.51 = f32[128,256]{1,0:T(8,128)} fusion(bf16[128,4096]{1,0:T(8,128)(2,1)} %all-gather.2.cloned.1.call-done, bf16[256,4096]{1,0:T(8,128)(2,1)S(1)} %copy-done), kind=kOutput, calls=%fused_computation.71 | convolution fusion | flops 268435456 | bytes 3276800 | tf_op jit(solution)/shard_map/dot_general | solution.py:54
  64.5 9.4 %reduce-scatter.3.cloned.1.call-done = f32[64,256]{1,0:T(8,128)} async-done(((f32[128,256]{1,0:T(8,128)}), f32[64,256]{1,0:T(8,128)}) %reduce-scatter.3.cloned.1.call-update) | async-done | bytes 65552 | tf_op jit(solution)/shard_map/reduce_scatter | solution.py:59
  73.9 0.9 multiply_reduce_fusion
  74.9 32.9 %psum.7 = f32[64]{0:T(128)S(1)} all-reduce(f32[64]{0:T(128)S(1)} %multiply_reduce_fusion), channel_id=1, replica_groups=mesh['expert'=16,'tensor'=2] {'expert'}, use_global_device_ids=true, to_apply=%region_8.9 | all-reduce | flops 64 | bytes 512 | tf_op jit(solution)/shard_map/psum | solution.py:61
  107.8 1.5 multiply_convert_fusion
  109.3 4.6 %all_gather.7 = bf16[128,256]{1,0:T(8,128)(2,1)S(1)} all-gather(bf16[64,256]{1,0:T(8,128)(2,1)S(1)} %get-tuple-element.2), channel_id=1, replica_groups=mesh['expert'=16,'tensor'=2] {'tensor'}, dimensions={0}, use_global_device_ids=true | all-gather | bytes 98304 | tf_op jit(solution)/shard_map/all_gather | solution.py:68
  113.9 9.0 %gather_fusion = bf16[2048,256]{1,0:T(8,128)(2,1)} fusion(bf16[128,256]{1,0:T(8,128)(2,1)S(1)} %all_gather.7, s32[2048]{0:T(1024)S(1)} %maximum_clamp_fusion), kind=kCustom, calls=%fused_computation | custom fusion | bytes 2105344 | tf_op jit(solution)/shard_map/gather | solution.py:89
  122.9 1.6 copy.39
  124.5 0.1 broadcast_select_fusion
  124.6 27.3 %all_to_all.44 = bf16[16,128,256]{1,2,0:T(8,128)(2,1)S(1)} all-to-all(bf16[16,128,256]{1,2,0:T(8,128)(2,1)S(1)} %broadcast_select_fusion), channel_id=1, replica_groups=mesh['expert'=16,'tensor'=2] {'expert'}, dimensions={0} | all-to-all | bytes 2097152 | tf_op jit(solution)/shard_map/all_to_all | solution.py:91
  151.9 5.0 %fusion.5 = f32[128,768]{1,0:T(8,128)S(1)} fusion(bf16[128,4096]{0,1:T(8,128)(2,1)S(1)} %bitcast.72, bf16[1,768,4096]{2,1,0:T(8,128)(2,1)} %param.21), kind=kOutput, calls=%fused_computation.8 | convolution fusion | flops 805306368 | bytes 7733248 | tf_op jit(solution)/shard_map/ecd,efd->ecf/dot_general | solution.py:92
  156.9 9.5 %fusion.10 = bf16[1,128,4096]{2,1,0:T(8,128)(2,1)} fusion(bf16[1,768,4096]{2,1,0:T(8,128)(2,1)} %param.23, bf16[128,4096]{0,1:T(8,128)(2,1)S(1)} %bitcast.73, bf16[1,768,4096]{2,1,0:T(8,128)(2,1)} %param.22, f32[128,768]{1,0:T(8,128)S(1)} %fusion.5), kind=kOutput, calls=%fused_computation.11 | convolution fusion | flops 1611726848 | bytes 15073280 | tf_op jit(solution)/shard_map/ecf,efd->ecd/dot_general | solution.py:95
  166.3 5.5 %copy.40 = bf16[1,128,4096]{1,0,2:T(2,128)(2,1)} copy(bf16[1,128,4096]{2,1,0:T(8,128)(2,1)} %fusion.10) | data formatting | bytes 2097152 | tf_op jit(solution)/shard_map/convert_element_type | solution.py:97
  171.9 0.5 broadcast.114
  172.4 23.4 %reduce = bf16[4096,128]{1,0:T(8,128)(2,1)S(1)} reduce(bf16[4096,1,128]{2,1,0:T(2,128)(2,1)} %bitcast.74, bf16[]{:T(256)} %broadcast.114), dimensions={1}, to_apply=%bitcast.63.reduce_sub_computation | reduce | bytes 2097154
  195.8 1.1 reshape.178
  197.0 4.9 %all-to-all-start.2 = ((bf16[16,2,16384]{2,1,0:T(2,128)(2,1)}), bf16[16,2,16384]{2,1,0:T(2,128)(2,1)S(1)}, u32[]{:S(2)}, u32[]{:S(2)}) async-start(bf16[16,2,16384]{2,1,0:T(2,128)(2,1)} %reshape.178), calls=%async_computation.3 | async-start | bytes 2097152 | tf_op jit(solution)/shard_map/all_to_all | solution.py:96
  201.9 0.0 reduce-scatter.5.cloned.1.call-start
  202.0 0.1 copy.42
  202.1 22.7 %all-to-all-done.2 = bf16[16,2,16384]{2,1,0:T(2,128)(2,1)S(1)} async-done(((bf16[16,2,16384]{2,1,0:T(2,128)(2,1)}), bf16[16,2,16384]{2,1,0:T(2,128)(2,1)S(1)}, u32[]{:S(2)}, u32[]{:S(2)}) %all-to-all-start.2) | async-done | bytes 1048608 | tf_op jit(solution)/shard_map/all_to_all | solution.py:96
  224.8 3.5 %reshape.179 = bf16[4096,1,128]{2,1,0:T(2,128)(2,1)} reshape(bf16[16,2,16384]{2,1,0:T(2,128)(2,1)S(1)} %all-to-all-done.2) | data formatting | bytes 2097152
  228.2 4.8 %bitcast_convert_fusion = f32[1,128,4096]{1,0,2:T(1,128)} fusion(bf16[4096,1,128]{2,1,0:T(2,128)(2,1)} %reshape.179), kind=kLoop, calls=%fused_computation.70 | loop fusion | flops 524288 | bytes 3145728 | tf_op jit(solution)/shard_map/convert_element_type | solution.py:98
  233.0 2.9 %copy.41 = f32[1,128,16,256]{3,1,2,0:T(8,128)} copy(f32[1,128,16,256]{1,3,2,0:T(8,128)} %bitcast.75) | data formatting | bytes 4194304 | tf_op jit(solution)/shard_map/convert_element_type | solution.py:98
  235.9 5.1 %gather_fusion.1 = f32[1024,256]{1,0:T(8,128)S(1)} fusion(f32[2048,256]{1,0:T(8,128)} %bitcast.71, s32[1024]{0:T(1024)S(1)} %broadcast_clamp_fusion), kind=kCustom, calls=%fused_computation.1 | custom fusion | bytes 2101248 | tf_op jit(solution)/shard_map/gather | solution.py:100
  241.0 1.0 fusion.20
  242.0 11.4 %reduce-scatter.5.cloned.1.call-done = bf16[64,256]{1,0:T(8,128)(2,1)} async-done(((bf16[128,256]{1,0:T(8,128)(2,1)}), bf16[64,256]{1,0:T(8,128)(2,1)}) %reduce-scatter.5.cloned.1.call-update) | async-done | bytes 32784 | tf_op jit(solution)/shard_map/reduce_scatter | solution.py:104
  (26 shorter events, 0.3 us)
Async XLA Ops:
  7.2 54.5 %copy-start = (bf16[256,4096]{1,0:T(8,128)(2,1)S(1)}, bf16[256,4096]{1,0:T(8,128)(2,1)}, u32[]{:S(2)}) copy-start(bf16[256,4096]{1,0:T(8,128)(2,1)} %param.17) | copy-start | bytes 6291460
  7.2 57.3 %copy-start.3 = (bf16[256]{0:T(256)(128)(2,1)S(1)}, bf16[256]{0:T(256)(128)(2,1)}, u32[]{:S(2)}) copy-start(bf16[256]{0:T(256)(128)(2,1)} %param.18) | copy-start | bytes 1540
  7.2 66.7 %copy-start.1 = (bf16[64,256]{1,0:T(8,128)(2,1)S(1)}, bf16[64,256]{1,0:T(8,128)(2,1)}, u32[]{:S(2)}) copy-start(bf16[64,256]{1,0:T(8,128)(2,1)} %param.16) | copy-start | bytes 98308
  7.2 54.5 %all-gather.2.cloned.1.call-start = ((), (), s32[]{:S(2)}) async-start(), calls=%async_computation.5 | async-start | bytes 1114112 | tf_op jit(solution)/shard_map/all_gather | solution.py:55
  23.3 50.6 %reduce-scatter.3.cloned.1.call-start = ((), (), s32[]{:S(2)}) async-start(), calls=%async_computation.6 | async-start | bytes 196608 | tf_op jit(solution)/shard_map/reduce_scatter | solution.py:59
  166.3 35.6 %copy-start.2 = (bf16[128,8]{0,1:T(8,128)(2,1)S(1)}, bf16[128,8]{0,1:T(8,128)(2,1)}, u32[]{:S(2)}) copy-start(bf16[128,8]{0,1:T(8,128)(2,1)} %param.20) | copy-start | bytes 6148
  197.0 27.8 %all-to-all-start.2 = ((bf16[16,2,16384]{2,1,0:T(2,128)(2,1)}), bf16[16,2,16384]{2,1,0:T(2,128)(2,1)S(1)}, u32[]{:S(2)}, u32[]{:S(2)}) async-start(bf16[16,2,16384]{2,1,0:T(2,128)(2,1)} %reshape.178), calls=%async_computation.3 | async-start | bytes 2097152 | tf_op jit(solution)/shard_map/all_to_all | solution.py:96
  201.9 51.5 %reduce-scatter.5.cloned.1.call-start = ((), (), s32[]{:S(2)}) async-start(), calls=%async_computation.7 | async-start | bytes 98304 | tf_op jit(solution)/shard_map/reduce_scatter | solution.py:104
Sparse Core Ops, SparseCore 0:
  23.4 38.2 all-gather.1
  64.6 9.3 reduce-scatter.2
  242.1 11.2 reduce-scatter.4
where the time goes:
time: 261 us; the launch traced here: 260 us
  blocking collectives  73 us (28%)
  waiting for transfers between devices  70.7 us (27%)
  other arithmetic  40.5 us (16%)
  local copies, waits for them, and re-layouts  36.7 us (14%)
  matrix products  20.1 us (8%)
  between operations  13.9 us (5%)
  starting transfers between devices  5.03 us (2%)
    psum x1, blocking collectives, body(): squares = lax.psum(jnp.sum(hidden_state * hidden_state, axis=1), 'expert')  32.9 us
    all_to_all x1, blocking collectives, body(): lax.all_to_all(outgoing, 'expert', split_axis=0, concat_axis=2, tiled=True)  27.3 us
    all_gather x1, waiting for transfers between devices, body(): lax.all_gather(context, 'expert', axis=0, tiled=True)  27.2 us
    unnamed x1, other arithmetic  23.4 us
    all_to_all x1, waiting for transfers between devices, body(): lax.all_to_all(result.astype(jnp.bfloat16), 'expert', split_axis=2, conca...  22.7 us
    reduce_scatter x1, waiting for transfers between devices, body(): lax.psum_scatter(mixed_rows.astype(jnp.bfloat16), 'tensor', scatter_dimen...  11.4 us
    gather x2, local copies, waits for them, and re-layouts, body(): normed[jnp.maximum(slot_owner, 0)]  10.6 us
    dot_general x1, matrix products, body(): jnp.einsum('ecf,efd->ecd', activation, w_down, preferred_element_type=jnp...  9.47 us
  transfers between devices with their start and end apart: 4, of which 4 were waited for; matrix products, arithmetic and copies ran while one was open for 4% of the time, Pallas kernels for 0%

commit v1 on v0

--- a/solution.py
+++ b/solution.py
@@ -2,9 +2,6 @@
 import jax.numpy as jnp
 from jax import lax
 from jax.sharding import PartitionSpec as P
-
-CAP = 128
-
 
 floor_value = -1e30
 epsilon = 1e-06
@@ -60,50 +57,32 @@
     hidden_state = residual.astype(jnp.float32) + attn_share
     squares = lax.psum(jnp.sum(hidden_state * hidden_state, axis=1), "expert")
     full_width = hidden_state.shape[1] * lax.axis_size("expert")
-    normed_share = (
-        hidden_state
-        * lax.rsqrt(squares[:, None] / full_width + epsilon)
-        * norm_gain.astype(jnp.float32)[None, :]
-    ).astype(jnp.bfloat16)
-    normed = lax.all_gather(normed_share, "tensor", axis=0, tiled=True)
+    scaled_share = (hidden_state * norm_gain.astype(jnp.float32)[None, :]).astype(jnp.bfloat16)
+    scaled = lax.all_gather(
+        lax.all_gather(scaled_share, "tensor", axis=0, tiled=True), "expert", axis=1, tiled=True
+    )
+    mean_all = lax.all_gather(squares / full_width, "tensor", axis=0, tiled=True)
+    row_scale = lax.rsqrt(mean_all + epsilon)[:, None]
     experts_local = w_gate.shape[0]
-    expert_count = experts_local * lax.axis_size("expert")
-    rows_all, choose_count = expert_ids.shape
-    flat_ids = expert_ids.reshape(-1)
-    onehot = (flat_ids[:, None] == jnp.arange(expert_count, dtype=jnp.int32)[None, :]).astype(
-        jnp.int32
-    )
-    slot_index = jnp.sum((jnp.cumsum(onehot, axis=0) - onehot) * onehot, axis=1)
-    destination = flat_ids * CAP + slot_index
-    source = jnp.arange(rows_all * choose_count, dtype=jnp.int32) // choose_count
-    slot_owner = (
-        jnp.full((expert_count * CAP,), -1, jnp.int32)
-        .at[destination]
-        .set(source)
-        .reshape(expert_count, CAP)
-    )
     gate_weight = gate_scores.astype(jnp.float32)
     gate_weight = gate_weight / jnp.sum(gate_weight, axis=1, keepdims=True)
-    filled = slot_owner >= 0
-    outgoing = jnp.where(
-        filled[..., None], normed[jnp.maximum(slot_owner, 0)], jnp.zeros((), jnp.bfloat16)
+    mixed = None
+    for local in range(experts_local):
+        expert = lax.axis_index("expert") * experts_local + local
+        weight = jnp.sum(jnp.where(expert_ids == expert, gate_weight, 0.0), axis=1, keepdims=True)
+        gate_proj = row_scale * lax.dot_general(
+            scaled, w_gate[local], (((1,), (1,)), ((), ())), preferred_element_type=jnp.float32
+        )
+        up_proj = row_scale * lax.dot_general(
+            scaled, w_up[local], (((1,), (1,)), ((), ())), preferred_element_type=jnp.float32
+        )
+        activation = (jax.nn.silu(gate_proj) * up_proj).astype(jnp.bfloat16)
+        part = weight * jnp.dot(activation, w_down[local], preferred_element_type=jnp.float32)
+        mixed = part if mixed is None else mixed + part
+    mixed = lax.psum_scatter(
+        mixed.astype(jnp.bfloat16), "tensor", scatter_dimension=0, tiled=True
     )
-    arrived = lax.all_to_all(outgoing, "expert", split_axis=0, concat_axis=2, tiled=True)
-    gate_proj = jnp.einsum("ecd,efd->ecf", arrived, w_gate, preferred_element_type=jnp.float32)
-    up_proj = jnp.einsum("ecd,efd->ecf", arrived, w_up, preferred_element_type=jnp.float32)
-    activation = (jax.nn.silu(gate_proj) * up_proj).astype(jnp.bfloat16)
-    result = jnp.einsum("ecf,efd->ecd", activation, w_down, preferred_element_type=jnp.float32)
-    returned = lax.all_to_all(
-        result.astype(jnp.bfloat16), "expert", split_axis=2, concat_axis=0, tiled=True
-    ).astype(result.dtype)
-    result_table = returned.reshape(expert_count * CAP, returned.shape[2])
-    gathered = result_table[destination]
-    mixed_rows = jnp.sum(
-        gathered.reshape(rows_all, choose_count, -1) * gate_weight[:, :, None], axis=1
-    )
-    mixed_share = lax.psum_scatter(
-        mixed_rows.astype(jnp.bfloat16), "tensor", scatter_dimension=0, tiled=True
-    )
+    mixed_share = lax.psum_scatter(mixed, "expert", scatter_dimension=1, tiled=True)
     return (hidden_state.astype(jnp.bfloat16), mixed_share)
 
 

time: 261 us -> 219 us (0.84)
  waiting for transfers between devices: 70.7 us -> 126 us
  other arithmetic: 40.5 us -> 5.06 us
  local copies, waits for them, and re-layouts: 36.7 us -> 2.19 us
  blocking collectives: 73 us -> 49.7 us
  starting transfers between devices: 5.03 us -> 0.2 us
    reduce_scatter x1 -> x2, waiting for transfers between devices: 11.4 us -> 78.7 us  [the longest x1 60.1 us: body(): lax.psum_scatter(mixed, 'expert', scatter_dimension=1, tiled=True)]
    all_to_all x1 -> x0, blocking collectives: 27.3 us -> none  [body(): lax.all_to_all(outgoing, 'expert', split_axis=0, concat_axis=2, tiled=True)]
    unnamed x1, other arithmetic: 23.4 us -> 0.09 us
    all_to_all x1 -> x0, waiting for transfers between devices: 22.7 us -> none  [body(): lax.all_to_all(result.astype(jnp.bfloat16), 'expert', split_axis=2, conca...]
    gather x3 -> x0, local copies, waits for them, and re-layouts: 15.7 us -> none  [the longest x2 10.6 us: body(): normed[jnp.maximum(slot_owner, 0)]]
    all_gather x1, waiting for transfers between devices: 27.2 us -> 38.2 us  [body(): lax.all_gather(context, 'expert', axis=0, tiled=True)]
    convert_element_type x2 -> x0, local copies, waits for them, and re-layouts: 8.43 us -> none  [the longest x1 5.54 us: body(): result.astype(jnp.bfloat16)]
    convert_element_type x3 -> x0, other arithmetic: 6.27 us -> none  [the longest x1 4.8 us: body(): returned = lax.all_to_all(result.astype(jnp.bfloat16), 'expert', split_ax...]
  transfers between devices with their start and end apart: 4 -> 5, of which waited for: 4 -> 4; matrix products, arithmetic and copies ran while one was open for 4% -> 0% of each run, Pallas kernels for 0% -> 0%
where the time goes in v1:
time: 219 us
  waiting for transfers between devices  126 us (58%)
  blocking collectives  49.7 us (23%)
  matrix products  20.7 us (9%)
  between operations  14.6 us (7%)
  other arithmetic  5.06 us (2%)
  local copies, waits for them, and re-layouts  2.19 us (1%)
    reduce_scatter x1, waiting for transfers between devices, body(): lax.psum_scatter(mixed, 'expert', scatter_dimension=1, tiled=True)  60.1 us
    all_gather x1, waiting for transfers between devices, body(): lax.all_gather(context, 'expert', axis=0, tiled=True)  38.2 us
    psum x1, blocking collectives, body(): squares = lax.psum(jnp.sum(hidden_state * hidden_state, axis=1), 'expert')  31.9 us
    reduce_scatter x1, waiting for transfers between devices, body(): lax.psum_scatter(mixed.astype(jnp.bfloat16), 'tensor', scatter_dimension=...  18.6 us
    dot_general x1, matrix products, body(): jnp.dot(activation, w_down[local], preferred_element_type=jnp.float32)  9.66 us
    reduce_scatter x1, waiting for transfers between devices, body(): lax.psum_scatter(attn_part, 'tensor', scatter_dimension=0, tiled=True)  9.44 us
    all_to_all x1, blocking collectives, body(): lax.all_to_all(context_rows_own, 'tensor', split_axis=1, concat_axis=0, t...  8.18 us
    dot_general x1, matrix products, body(): lax.dot_general(scaled, w_gate[local], (((1,), (1,)), ((), ())), preferre...  5.4 us
  transfers between devices with their start and end apart: 5, of which 4 were waited for; matrix products, arithmetic and copies ran while one was open for 0% of the time, Pallas kernels for 0%

profile of v1, /device:TPU:0, one launch (start us, length us, event | category | flops | bytes accessed | tf_op | source)
XLA Modules:
  0.0 218.9 jit_solution(551768819832569103)
XLA Ops:
  7.2 0.0 copy-start
  7.2 0.0 copy-start.6
  7.2 0.0 copy-start.5
  7.2 0.0 copy-start.2
  7.2 0.0 copy-start.3
  7.2 0.0 copy-start.4
  7.2 0.0 all-gather.3.cloned.1.call-start
  7.3 0.9 iota_compare_fusion
  8.1 0.8 copy.19
  9.0 1.5 select_reduce_fusion
  10.5 2.5 %fusion = f32[4,4,16,128]{3,2,1,0:T(8,128)S(1)} fusion(f32[4,4,16,128]{3,2,1,0:T(8,128)S(1)} %get-tuple-element.6, f32[4,4,16]{2,1,0:T(4,128)S(1)} %get-tuple-element.5, pred[4,128]{1,0:T(4,128)(4,1)S(1)} %iota_compare_fusion), kind=kOutput, calls=%fused_computation | output fusion | flops 65919 | bytes 263680 | tf_op jit(solution)/shard_map/div | solution.py:48
  13.0 1.4 fusion.25
  14.4 0.1 copy.18
  14.5 8.2 %all_to_all.19 = bf16[4,2,4096]{2,0,1:T(4,128)(2,1)S(1)} all-to-all(bf16[4,2,4096]{2,0,1:T(4,128)(2,1)S(1)} %copy.18), channel_id=1, replica_groups=mesh['expert'=16,'tensor'=2] {'tensor'}, dimensions={1} | all-to-all | bytes 131072 | tf_op jit(solution)/shard_map/all_to_all | solution.py:50
  22.7 0.6 all_to_all.17
  23.3 0.0 all-gather.3.cloned.1.call-update
  23.3 0.0 reduce-scatter.4.cloned.1.call-start
  23.4 38.2 %all-gather.3.cloned.1.call-done = bf16[128,4096]{1,0:T(8,128)(2,1)} async-done(((bf16[8,4096]{1,0:T(8,128)(2,1)}), bf16[128,4096]{1,0:T(8,128)(2,1)}) %all-gather.3.cloned.1.call-update) | async-done | bytes 1048592 | tf_op jit(solution)/shard_map/all_gather | solution.py:52
  61.6 0.0 copy-done
  61.6 2.7 %fusion.50 = f32[128,256]{1,0:T(8,128)} fusion(bf16[128,4096]{1,0:T(8,128)(2,1)} %all-gather.3.cloned.1.call-done, bf16[256,4096]{1,0:T(8,128)(2,1)S(1)} %copy-done), kind=kOutput, calls=%fused_computation.48 | convolution fusion | flops 268435456 | bytes 3276800 | tf_op jit(solution)/shard_map/dot_general | solution.py:51
  64.3 0.0 reduce-scatter.4.cloned.1.call-update
  64.3 0.0 all-gather.5.cloned.1.call-start
  64.4 0.0 copy-done.5
  64.4 9.4 %reduce-scatter.4.cloned.1.call-done = f32[64,256]{1,0:T(8,128)} async-done(((f32[128,256]{1,0:T(8,128)}), f32[64,256]{1,0:T(8,128)}) %reduce-scatter.4.cloned.1.call-update) | async-done | bytes 65552 | tf_op jit(solution)/shard_map/reduce_scatter | solution.py:56
  73.8 0.0 copy-done.2
  73.8 1.6 multiply_reduce_fusion
  75.4 4.7 %all_gather.14 = bf16[128,256]{1,0:T(8,128)(2,1)} all-gather(bf16[64,256]{1,0:T(8,128)(2,1)S(1)} %get-tuple-element.3), channel_id=1, replica_groups=mesh['expert'=16,'tensor'=2] {'tensor'}, dimensions={0}, use_global_device_ids=true | all-gather | bytes 98304 | tf_op jit(solution)/shard_map/all_gather | solution.py:62
  80.1 0.0 all-gather.5.cloned.1.call-update
  80.1 0.0 reduce-scatter.6.cloned.1.call-start
  80.2 0.0 copy-done.6
  80.2 0.6 dynamic-slice
  81.4 0.0 copy-done.3
  81.5 0.0 copy-done.4
  81.5 31.9 %psum.7 = f32[64]{0:T(128)S(1)} all-reduce(f32[64]{0:T(128)S(1)} %get-tuple-element.2), channel_id=1, replica_groups=mesh['expert'=16,'tensor'=2] {'expert'}, use_global_device_ids=true, to_apply=%region_6.7 | all-reduce | flops 64 | bytes 512 | tf_op jit(solution)/shard_map/psum | solution.py:58
  113.4 0.1 multiply_dynamic-update-slice_fusion
  113.5 4.9 %all-reduce = f32[128]{0:T(128)S(1)} all-reduce(f32[128]{0:T(128)S(1)} %multiply_dynamic-update-slice_fusion), channel_id=1, replica_groups=mesh['expert'=16,'tensor'=2] {'tensor'}, use_global_device_ids=true, to_apply=%add | all-reduce | flops 128 | bytes 1024
  118.5 0.0 all-gather.5.cloned.1.call-done
  118.5 0.0 copy-start.1
  118.5 5.4 %fusion.13 = f32[128,768]{1,0:T(8,128)S(1)} fusion(bf16[128,4096]{1,0:T(8,128)(2,1)} %all-gather.5.cloned.1.call-done, bf16[1,768,4096]{2,1,0:T(8,128)(2,1)} %param.21, f32[128]{0:T(128)S(1)} %add_rsqrt_fusion), kind=kOutput, calls=%fused_computation.9 | convolution fusion | flops 805404672 | bytes 7733760 | tf_op jit(solution)/shard_map/dot_general | solution.py:73
  123.9 0.0 copy-done.1
  123.9 9.7 %fusion.10 = bf16[128,4096]{1,0:T(8,128)(2,1)} fusion(bf16[1,768,4096]{2,1,0:T(8,128)(2,1)} %param.23, f32[128]{0:T(128)S(1)} %fusion.46, bf16[128,4096]{1,0:T(8,128)(2,1)S(1)} %copy-done.1, bf16[1,768,4096]{2,1,0:T(8,128)(2,1)} %param.22, f32[128,768]{1,0:T(8,128)S(1)} %fusion.13, f32[128]{0:T(128)S(1)} %add_rsqrt_fusion), kind=kOutput, calls=%fused_computation.8 | convolution fusion | flops 1612349440 | bytes 15074304 | tf_op jit(solution)/shard_map/dot_general | solution.py:80
  133.5 0.0 reduce-scatter.6.cloned.1.call-update
  133.6 0.0 reduce-scatter.8.cloned.1.call-start
  133.6 18.6 %reduce-scatter.6.cloned.1.call-done = bf16[64,4096]{1,0:T(8,128)(2,1)} async-done(((bf16[128,4096]{1,0:T(8,128)(2,1)}), bf16[64,4096]{1,0:T(8,128)(2,1)}) %reduce-scatter.6.cloned.1.call-update) | async-done | bytes 524304 | tf_op jit(solution)/shard_map/reduce_scatter | solution.py:82
  152.2 0.0 reduce-scatter.8.cloned.1.call-update
  152.2 60.1 %reduce-scatter.8.cloned.1.call-done = bf16[64,256]{1,0:T(8,128)(2,1)} async-done(((bf16[64,4096]{1,0:T(8,128)(2,1)}), bf16[64,256]{1,0:T(8,128)(2,1)}) %reduce-scatter.8.cloned.1.call-update) | async-done | bytes 32784 | tf_op jit(solution)/shard_map/reduce_scatter | solution.py:85
  (6 shorter events, 0.1 us)
Async XLA Ops:
  7.2 54.4 %copy-start = (bf16[256,4096]{1,0:T(8,128)(2,1)S(1)}, bf16[256,4096]{1,0:T(8,128)(2,1)}, u32[]{:S(2)}) copy-start(bf16[256,4096]{1,0:T(8,128)(2,1)} %param.17) | copy-start | bytes 6291460
  7.2 73.0 %copy-start.6 = (u32[32]{0:T(128)S(1)}, u32[32]{0:T(128)}, u32[]{:S(2)}) copy-start(u32[32]{0:T(128)} %constant.31) | copy-start | bytes 388
  7.2 57.2 %copy-start.5 = (bf16[256]{0:T(256)(128)(2,1)S(1)}, bf16[256]{0:T(256)(128)(2,1)}, u32[]{:S(2)}) copy-start(bf16[256]{0:T(256)(128)(2,1)} %param.18) | copy-start | bytes 1540
  7.2 66.6 %copy-start.2 = (bf16[64,256]{1,0:T(8,128)(2,1)S(1)}, bf16[64,256]{1,0:T(8,128)(2,1)}, u32[]{:S(2)}) copy-start(bf16[64,256]{1,0:T(8,128)(2,1)} %param.16) | copy-start | bytes 98308
  7.2 74.2 %copy-start.3 = (bf16[128,8]{0,1:T(8,128)(2,1)S(1)}, bf16[128,8]{0,1:T(8,128)(2,1)}, u32[]{:S(2)}) copy-start(bf16[128,8]{0,1:T(8,128)(2,1)} %param.20) | copy-start | bytes 6148
  7.2 74.2 %copy-start.4 = (s32[128,8]{0,1:T(8,128)S(1)}, s32[128,8]{0,1:T(8,128)}, u32[]{:S(2)}) copy-start(s32[128,8]{0,1:T(8,128)} %param.19) | copy-start | bytes 12292
  7.2 54.4 %all-gather.3.cloned.1.call-start = ((), (), s32[]{:S(2)}) async-start(), calls=%async_computation.4 | async-start | bytes 1114112 | tf_op jit(solution)/shard_map/all_gather | solution.py:52
  23.3 50.5 %reduce-scatter.4.cloned.1.call-start = ((), (), s32[]{:S(2)}) async-start(), calls=%async_computation.5 | async-start | bytes 196608 | tf_op jit(solution)/shard_map/reduce_scatter | solution.py:56
  64.3 54.1 %all-gather.5.cloned.1.call-start = ((), (), s32[]{:S(2)}) async-start(), calls=%async_computation.6 | async-start | bytes 1114112 | tf_op jit(solution)/shard_map/all_gather | solution.py:61
  80.1 72.1 %reduce-scatter.6.cloned.1.call-start = ((), (), s32[]{:S(2)}) async-start(), calls=%async_computation.7 | async-start | bytes 1572864 | tf_op jit(solution)/shard_map/reduce_scatter | solution.py:82
  118.5 5.4 %copy-start.1 = (bf16[128,4096]{1,0:T(8,128)(2,1)S(1)}, bf16[128,4096]{1,0:T(8,128)(2,1)}, u32[]{:S(2)}) copy-start(bf16[128,4096]{1,0:T(8,128)(2,1)} %all-gather.5.cloned.1.call-done) | copy-start | bytes 3145732
  133.6 78.8 %reduce-scatter.8.cloned.1.call-start = ((), (), s32[]{:S(2)}) async-start(), calls=%async_computation.8 | async-start | bytes 557056 | tf_op jit(solution)/shard_map/reduce_scatter | solution.py:85
Sparse Core Ops, SparseCore 0:
  23.4 38.1 all-gather.2
  64.5 9.3 reduce-scatter.3
  80.3 36.6 all-gather.4
  133.7 18.4 reduce-scatter.5
  156.2 56.1 reduce-scatter.7

commit v2 on v1

--- a/solution.py
+++ b/solution.py
@@ -1,6 +1,8 @@
 import jax
 import jax.numpy as jnp
 from jax import lax
+from jax.experimental import pallas as pl
+from jax.experimental.pallas import tpu as pltpu
 from jax.sharding import PartitionSpec as P
 
 floor_value = -1e30
@@ -86,6 +88,405 @@
     return (hidden_state.astype(jnp.bfloat16), mixed_share)
 
 
+MESH = pl.DeviceIdType.MESH
+NZ = 4
+UP, DOWN, ACROSS, CORE = 0, 3, 6, 10
+
+
+def remote(src, dst, send, recv, device):
+    return pltpu.make_async_remote_copy(
+        src_ref=src, dst_ref=dst, send_sem=send, recv_sem=recv, device_id=device, device_id_type=MESH
+    )
+
+
+class Gather:
+    def __init__(self, bufs, sends, recvs, e, y):
+        self.bufs, self.sends, self.recvs = bufs, sends, recvs
+        self.e, self.y = e, y
+        self.z, self.x, self.c = e // 4, (e // 2) % 2, e % 2
+        self.ex = e + 2 * (1 - 2 * self.x)
+        self.ec = e + 1 - 2 * self.c
+
+    def copies(self, slot, sem, target):
+        return [
+            remote(
+                b.at[slot], b.at[slot], self.sends.at[i, sem], self.recvs.at[i, sem], (target, self.y)
+            )
+            for i, b in enumerate(self.bufs)
+        ]
+
+    def start(self, slot, sem, target):
+        for d in self.copies(slot, sem, target):
+            d.start()
+
+    def landed(self, slot, sem):
+        for d in self.copies(slot, sem, self.ec):
+            d.wait_recv()
+
+    def sent(self, slot, sem):
+        for d in self.copies(slot, sem, self.ec):
+            d.wait_send()
+
+    def slot(self, zz, xx, cc):
+        return zz * 4 + xx * 2 + cc
+
+    def forward(self, slot, zz):
+        self.start(slot, ACROSS + zz, self.ex)
+        self.start(slot, CORE + self.x * NZ + zz, self.ec)
+
+    def run(self):
+        z, x, c, e = self.z, self.x, self.c, self.e
+
+        @pl.when(z < NZ - 1)
+        def _():
+            self.start(e, UP, e + 4)
+
+        @pl.when(z > 0)
+        def _():
+            self.start(e, DOWN, e - 4)
+
+        self.forward(e, z)
+        for k in range(1, NZ):
+
+            @pl.when(z - k >= 0)
+            def _(k=k):
+                slot = e - 4 * k
+                self.landed(slot, UP + k - 1)
+                if k < NZ - 1:
+
+                    @pl.when(z < NZ - 1)
+                    def _():
+                        self.start(slot, UP + k, e + 4)
+
+                self.forward(slot, z - k)
+
+            @pl.when(z + k <= NZ - 1)
+            def _(k=k):
+                slot = e + 4 * k
+                self.landed(slot, DOWN + k - 1)
+                if k < NZ - 1:
+
+                    @pl.when(z > 0)
+                    def _():
+                        self.start(slot, DOWN + k, e - 4)
+
+                self.forward(slot, z + k)
+
+        step = 1 - 2 * (z // 2)
+        for j in range(NZ):
+            zz = (z + step * j + NZ) % NZ
+            slot = self.slot(zz, 1 - x, c)
+            self.landed(slot, ACROSS + zz)
+            self.start(slot, CORE + (1 - x) * NZ + zz, self.ec)
+
+    def wait_core(self):
+        for xx in range(2):
+            for zz in range(NZ):
+                self.landed(self.slot(zz, xx, 1 - self.c), CORE + xx * NZ + zz)
+
+    def wait_sends(self):
+        z, e = self.z, self.e
+        for k in range(1, NZ):
+
+            @pl.when((z < NZ - 1) & (z - (k - 1) >= 0))
+            def _(k=k):
+                self.sent(e - 4 * (k - 1), UP + k - 1)
+
+            @pl.when((z > 0) & (z + k - 1 <= NZ - 1))
+            def _(k=k):
+                self.sent(e + 4 * (k - 1), DOWN + k - 1)
+
+        for zz in range(NZ):
+            self.sent(self.slot(zz, self.x, self.c), ACROSS + zz)
+            for xx in range(2):
+                self.sent(self.slot(zz, xx, self.c), CORE + xx * NZ + zz)
+
+
+def nt_dot(a, b):
+    return lax.dot_general(a, b, (((1,), (1,)), ((), ())), preferred_element_type=jnp.float32)
+
+
+def layer_kernel(
+    q_ref, k_hbm, v_hbm, len_ref, res_ref, wo_hbm, gain_ref, ids_ref, gates_ref,
+    wg_hbm, wu_hbm, wd_hbm,
+    hid_ref, mix_ref,
+    k_v, v_v, wo_v, wg_v, wu_v, wd_v, local_sems,
+    lay, qlay, sblk, ctx, part, part_in, hid_all, sq_all,
+    gate_acc, up_acc, act, own, tmp, core_in, xout, x_in, zout, up_in, down_in, yout, y_in,
+    c_send, c_recv, h_send, h_recv, p_send, p_recv, r_send, r_recv,
+):
+    f32, bf16 = jnp.float32, jnp.bfloat16
+    e = lax.axis_index("expert")
+    y = lax.axis_index("tensor")
+    z, x, c = e // 4, (e // 2) % 2, e % 2
+    ex, ec = e + 2 * (1 - 2 * x), e + 1 - 2 * c
+    barrier = pltpu.get_barrier_semaphore()
+    pairs = [(k_hbm, k_v), (v_hbm, v_v), (wo_hbm, wo_v), (wg_hbm, wg_v), (wu_hbm, wu_v), (wd_hbm, wd_v)]
+    loads = [pltpu.make_async_copy(s, d, local_sems.at[i]) for i, (s, d) in enumerate(pairs)]
+    for d in loads:
+        d.start()
+    for dev in ((ec, y), (ex, y), (e, 1 - y)):
+        pl.semaphore_signal(barrier, inc=1, device_id=dev, device_id_type=MESH)
+
+    @pl.when(z > 0)
+    def _():
+        pl.semaphore_signal(barrier, inc=1, device_id=(e - 4, y), device_id_type=MESH)
+
+    @pl.when(z < NZ - 1)
+    def _():
+        pl.semaphore_signal(barrier, inc=1, device_id=(e + 4, y), device_id_type=MESH)
+
+    rows = q_ref.shape[0]
+    for h in range(64):
+        qlay[h * 8 : h * 8 + rows, :] = q_ref[:, h * 128 : (h + 1) * 128].astype(f32)
+    loads[0].wait()
+    loads[1].wait()
+    col = lax.broadcasted_iota(jnp.int32, (64, 512), 1)
+    head = lax.broadcasted_iota(jnp.int32, (64, 512), 0)
+    same = (col % 4) == (head // 16)
+    for r in range(rows):
+        q = qlay[pl.ds(r, 64, stride=8), :].astype(bf16)
+        s = nt_dot(q, k_v[r]) * (128 ** -0.5)
+        ok = same & ((col // 4) < len_ref[r])
+        peak = jnp.max(jnp.where(ok, s, -1e30), axis=1, keepdims=True)
+        w = jnp.where(ok, jnp.exp(s - peak), 0.0)
+        total = jnp.sum(w, axis=1, keepdims=True)
+        o = jnp.dot(w.astype(bf16), v_v[r], preferred_element_type=f32) / total
+        for half in range(2):
+            for j in range(4):
+                h0 = half * 32 + j * 8
+                lay[pl.ds(half * 128 + 4 * j + r, 8, stride=16), :] = o[h0 : h0 + 8]
+    for half in range(2):
+        for hh in range(8):
+            t = (half * 8 + hh) * 16
+            sblk[half, :, hh * 128 : (hh + 1) * 128] = lay[t : t + 16, :].astype(bf16)
+    ctx[e, y] = sblk[y]
+    pl.semaphore_wait(barrier, 4 + z * (NZ - 1 - z) // 2)
+
+    swap = remote(sblk.at[1 - y], ctx.at[e, y], p_send.at[0], p_recv.at[0], (e, 1 - y))
+    swap.start()
+    swap.wait_recv()
+    g1 = Gather([ctx], c_send, c_recv, e, y)
+    g1.run()
+    g1.wait_core()
+
+    loads[2].wait()
+    lhs = ctx.reshape(512, 1024)
+    quarter = (lax.broadcasted_iota(jnp.int32, (512, 256), 0) % 16) // 4
+    acc = jnp.zeros((512, 256), f32)
+    for j in range(4):
+        pj = nt_dot(lhs[...], wo_v[:, j * 1024 : (j + 1) * 1024])
+        acc = jnp.where(quarter == j, pj, acc)
+    folded = acc.reshape(32, 2, 8, 256)
+    folded = (folded[:, 0] + folded[:, 1]).reshape(256, 256)
+    low = (lax.broadcasted_iota(jnp.int32, (256, 256), 0) % 8) < 4
+    folded = folded + jnp.where(low, pltpu.roll(folded, 252, 0), pltpu.roll(folded, 4, 0))
+    folded = folded.reshape(16, 2, 8, 256)
+    low3 = lax.broadcasted_iota(jnp.int32, (16, 8, 256), 1) < 4
+    part[...] = jnp.where(low3, folded[:, 0], folded[:, 1]).reshape(2, 64, 256)
+    psend = remote(part.at[1 - y], part_in, p_send.at[1], p_recv.at[1], (e, 1 - y))
+    psend.start()
+    psend.wait_recv()
+    hidden = res_ref[...].astype(f32) + (part[y] + part_in[...])
+    hid_ref[...] = hidden.astype(bf16)
+    hid_all[e, y] = (hidden * gain_ref[...].astype(f32)).astype(bf16)
+    ss = jnp.sum(hidden * hidden, axis=1, keepdims=True)
+    place = lax.broadcasted_iota(jnp.int32, (64, 128), 0) + 64 * y
+    lane = lax.broadcasted_iota(jnp.int32, (64, 128), 1)
+    sq = jnp.sum(jnp.where(place == lane, ss, 0.0), axis=0, keepdims=True)
+    sq_all[e, y] = jnp.broadcast_to(sq, (8, 128))
+    hs = remote(hid_all.at[e, y], hid_all.at[e, y], p_send.at[2], p_recv.at[2], (e, 1 - y))
+    qs = remote(sq_all.at[e, y], sq_all.at[e, y], p_send.at[3], p_recv.at[3], (e, 1 - y))
+    hs.start()
+    qs.start()
+    hs.wait_recv()
+    qs.wait_recv()
+    g2 = Gather([hid_all, sq_all], h_send, h_recv, e, y)
+    g2.run()
+    loads[3].wait()
+    loads[4].wait()
+
+    def products(core, first):
+        def step(n, _):
+            rows_n = pl.ds(pl.multiple_of(n * 256, 256), 256)
+            for wref, aref in ((wg_v, gate_acc), (wu_v, up_acc)):
+                a = jnp.zeros((128, 256), f32) if first else aref[n]
+                for j in range(8):
+                    src = 2 * j + core
+                    cols = pl.ds(pl.multiple_of(src * 256, 256), 256)
+                    a = a + nt_dot(hid_all[src].reshape(128, 256), wref[rows_n, cols])
+                aref[n] = a
+            return 0
+
+        lax.fori_loop(0, 3, step, 0)
+
+    products(c, True)
+    g2.wait_core()
+    products(1 - c, False)
+    total = jnp.sum(sq_all[...].reshape(32, 8, 128), axis=0)
+    scale_row = lax.rsqrt(total[0:1] / 4096.0 + epsilon)
+    eye = lax.broadcasted_iota(jnp.int32, (128, 128), 0) == lax.broadcasted_iota(jnp.int32, (128, 128), 1)
+    scale = jnp.sum(jnp.where(eye, scale_row, 0.0), axis=1, keepdims=True)
+    gw = gates_ref[...].astype(f32)
+    gw = gw / jnp.sum(gw, axis=1, keepdims=True)
+    weight = jnp.sum(jnp.where(ids_ref[...] == e, gw, 0.0), axis=1, keepdims=True)
+    for n in range(3):
+        g = gate_acc[n] * scale
+        u = up_acc[n] * scale
+        act[:, n * 256 : (n + 1) * 256] = (g / (1.0 + jnp.exp(-g)) * u).astype(bf16)
+    loads[5].wait()
+
+    def block(zz, xx, cc):
+        cols = pl.ds(pl.multiple_of((zz * 4 + xx * 2 + cc) * 256, 256), 256)
+        return jnp.dot(act[...], wd_v[:, cols], preferred_element_type=f32) * weight
+
+    def core_copy(b):
+        return remote(tmp.at[b], core_in.at[b], r_send.at[b], r_recv.at[b], (ec, y))
+
+    def x_copy(b):
+        return remote(xout.at[b], x_in.at[b], r_send.at[8 + b], r_recv.at[8 + b], (ex, y))
+
+    def other_core(i, _):
+        xx = (1 - x + i // 4) % 2
+        b = xx * 4 + i % 4
+        tmp[b] = block(i % 4, xx, 1 - c).astype(bf16)
+        core_copy(b).start()
+        return 0
+
+    lax.fori_loop(0, 8, other_core, 0)
+
+    def far(zz, _):
+        p = block(zz, 1 - x, c)
+        b = (1 - x) * 4 + zz
+        core_copy(b).wait_recv()
+        xout[zz] = (p + core_in[b].astype(f32)).astype(bf16)
+        x_copy(zz).start()
+        return 0
+
+    lax.fori_loop(0, 4, far, 0)
+
+    def near(zz, _):
+        p = block(zz, x, c)
+        b = x * 4 + zz
+        core_copy(b).wait_recv()
+        own[zz] = p + core_in[b].astype(f32)
+        return 0
+
+    lax.fori_loop(0, 4, near, 0)
+
+    def x_done(zz, _):
+        x_copy(zz).wait_recv()
+        own[zz] = own[zz] + x_in[zz].astype(f32)
+        return 0
+
+    lax.fori_loop(0, 4, x_done, 0)
+
+    def up_copy(zz):
+        return remote(zout.at[zz], up_in.at[zz], r_send.at[12 + zz], r_recv.at[12 + zz], (e + 4, y))
+
+    def down_copy(zz):
+        return remote(zout.at[zz], down_in.at[zz], r_send.at[12 + zz], r_recv.at[16 + zz], (e - 4, y))
+
+    for k in range(NZ - 1, 0, -1):
+
+        @pl.when(z + k <= NZ - 1)
+        def _(k=k):
+            zz = z + k
+
+            @pl.when(z > 0)
+            def _():
+                up_copy(zz).wait_recv()
+                own[zz] = own[zz] + up_in[zz].astype(f32)
+
+            zout[zz] = own[zz].astype(bf16)
+            up_copy(zz).start()
+
+        @pl.when(z - k >= 0)
+        def _(k=k):
+            zz = z - k
+
+            @pl.when(z < NZ - 1)
+            def _():
+                down_copy(zz).wait_recv()
+                own[zz] = own[zz] + down_in[zz].astype(f32)
+
+            zout[zz] = own[zz].astype(bf16)
+            down_copy(zz).start()
+
+    @pl.when(z > 0)
+    def _():
+        up_copy(z).wait_recv()
+        own[z] = own[z] + up_in[z].astype(f32)
+
+    @pl.when(z < NZ - 1)
+    def _():
+        down_copy(z).wait_recv()
+        own[z] = own[z] + down_in[z].astype(f32)
+
+    final = own.at[z].reshape(2, 64, 256)
+    yout[...] = final[1 - y].astype(bf16)
+    ysend = remote(yout, y_in, p_send.at[4], p_recv.at[4], (e, 1 - y))
+    ysend.start()
+    ysend.wait_recv()
+    mix_ref[...] = (final[y] + y_in[...].astype(f32)).astype(bf16)
+
+    for d in (swap, psend, hs, qs, ysend):
+        d.wait_send()
+    g1.wait_sends()
+    g2.wait_sends()
+    for b in range(8):
+        core_copy(b).wait_send()
+    for b in range(4):
+        x_copy(b).wait_send()
+    for k in range(1, NZ):
+
+        @pl.when(z + k <= NZ - 1)
+        def _(k=k):
+            up_copy(z + k).wait_send()
+
+        @pl.when(z - k >= 0)
+        def _(k=k):
+            down_copy(z - k).wait_send()
+
+
+def fused_body(
+    query, cache_keys, cache_values, lengths, residual, out_proj, norm_gain, expert_ids, gate_scores,
+    w_gate, w_up, w_down,
+):
+    f32, bf16 = jnp.float32, jnp.bfloat16
+    rows = query.shape[0]
+    keys = cache_keys.reshape(rows, 512, 128)
+    values = cache_values.reshape(rows, 512, 128)
+    vm = pl.BlockSpec(memory_space=pltpu.VMEM)
+    hb = pl.BlockSpec(memory_space=pl.ANY)
+    sm = pl.BlockSpec(memory_space=pltpu.SMEM)
+    V, S = pltpu.VMEM, pltpu.SemaphoreType.DMA
+    return pl.pallas_call(
+        layer_kernel,
+        name="layer",
+        out_shape=(jax.ShapeDtypeStruct((64, 256), bf16), jax.ShapeDtypeStruct((64, 256), bf16)),
+        in_specs=[vm, hb, hb, sm, vm, hb, vm, vm, vm, hb, hb, hb],
+        out_specs=(vm, vm),
+        scratch_shapes=[
+            V((rows, 512, 128), bf16), V((rows, 512, 128), bf16), V((256, 4096), bf16),
+            V((768, 4096), bf16), V((768, 4096), bf16), V((768, 4096), bf16), S((6,)),
+            V((256, 128), f32), V((512, 128), f32), V((2, 16, 1024), bf16), V((16, 2, 16, 1024), bf16),
+            V((2, 64, 256), f32), V((64, 256), f32), V((16, 2, 64, 256), bf16), V((16, 2, 8, 128), f32),
+            V((3, 128, 256), f32), V((3, 128, 256), f32), V((128, 768), bf16),
+            V((4, 128, 256), f32), V((8, 128, 256), bf16), V((8, 128, 256), bf16),
+            V((4, 128, 256), bf16), V((4, 128, 256), bf16), V((4, 128, 256), bf16),
+            V((4, 128, 256), bf16), V((4, 128, 256), bf16), V((64, 256), bf16), V((64, 256), bf16),
+            S((1, 18)), S((1, 18)), S((2, 18)), S((2, 18)), S((5,)), S((5,)), S((20,)), S((20,)),
+        ],
+        compiler_params=pltpu.CompilerParams(
+            collective_id=0, has_side_effects=True, vmem_limit_bytes=62 * 1024 * 1024
+        ),
+    )(
+        query, keys, values, lengths, residual, out_proj, norm_gain.reshape(1, -1), expert_ids,
+        gate_scores, w_gate[0], w_up[0], w_down[0],
+    )
+
+
 def solution(mesh):
     in_specs = (
         P(("expert", "tensor"), None),
@@ -102,4 +503,5 @@
         P("expert", "tensor", None),
     )
     out_specs = (P("tensor", "expert"), P("tensor", "expert"))
-    return jax.shard_map(body, mesh=mesh, in_specs=in_specs, out_specs=out_specs, check_vma=False)
+    fused = dict(mesh.shape) == {"expert": 16, "tensor": 2}
+    return jax.shard_map(fused_body if fused else body, mesh=mesh, in_specs=in_specs, out_specs=out_specs, check_vma=False)

time: 219 us -> 81.2 us (0.37)
  waiting for transfers between devices: 126 us -> 0 us
  Pallas kernels: 0 us -> 73.4 us
  blocking collectives: 49.7 us -> 0 us
  matrix products: 20.7 us -> 0 us
  between operations: 14.6 us -> 0.64 us
  other arithmetic: 5.06 us -> 0 us
  local copies, waits for them, and re-layouts: 2.19 us -> 6.77 us
    reduce_scatter x3 -> x0, waiting for transfers between devices: 88.2 us -> none  [the longest x1 60.1 us: body(): lax.psum_scatter(mixed, 'expert', scatter_dimension=1, tiled=True)]
    pallas_call x0 -> x1, Pallas kernels: none -> 73.4 us  [fused_body(): pl.pallas_call(layer_kernel, name='layer', out_shape=(jax.ShapeDtypeStruc...]
    all_gather x2 -> x0, waiting for transfers between devices: 38.2 us -> none  [the longest x1 38.2 us: body(): lax.all_gather(context, 'expert', axis=0, tiled=True)]
    psum x1 -> x0, blocking collectives: 31.9 us -> none  [body(): squares = lax.psum(jnp.sum(hidden_state * hidden_state, axis=1), 'expert')]
    dot_general x5 -> x0, matrix products: 20.7 us -> none  [the longest x1 9.66 us: body(): jnp.dot(activation, w_down[local], preferred_element_type=jnp.float32)]
    all_to_all x1 -> x0, blocking collectives: 8.18 us -> none  [body(): lax.all_to_all(context_rows_own, 'tensor', split_axis=1, concat_axis=0, t...]
    unnamed x1 -> x0, blocking collectives: 4.91 us -> none
    all_gather x1 -> x0, blocking collectives: 4.69 us -> none  [body(): lax.all_gather(scaled_share, 'tensor', axis=0, tiled=True)]
  transfers between devices with their start and end apart: 5 -> 0, of which waited for: 4 -> 0; matrix products, arithmetic and copies ran while one was open for 0% -> 0% of each run, Pallas kernels for 0% -> 0%
where the time goes in v2:
time: 81.2 us; the launch traced here: 80.8 us
  Pallas kernels  73.4 us (90%)
  local copies, waits for them, and re-layouts  6.77 us (8%)
    pallas_call x1, Pallas kernels, fused_body(): pl.pallas_call(layer_kernel, name='layer', out_shape=(jax.ShapeDtypeStruc...  73.4 us
    unnamed x4, local copies, waits for them, and re-layouts  5.55 us

profile of v2, /device:TPU:0, one launch (start us, length us, event | category | flops | bytes accessed | tf_op | source)
XLA Modules:
  0.0 80.8 jit_solution(4747371666505300707)
XLA Ops:
  0.6 1.2 %reshape.15.gain_ref = bf16[1,256]{1,0:T(2,128)(2,1)} reshape(bf16[256]{0:T(256)(128)(2,1)} %param.18) | data formatting | bytes 1024 | tf_op jit(solution)/shard_map/reshape | solution.py:485
  1.8 1.4 %copy.15.gates_ref = bf16[128,8]{1,0:T(8,128)(2,1)} copy(bf16[128,8]{0,1:T(8,128)(2,1)} %param.20) | data formatting | bytes 4096 | tf_op args[8]
  3.2 1.4 %copy.14.ids_ref = s32[128,8]{1,0:T(8,128)} copy(s32[128,8]{0,1:T(8,128)} %param.19) | data formatting | bytes 8192 | tf_op args[7]
  4.7 73.4 %layer.1 = (bf16[64,256]{1,0:T(8,128)(2,1)}, bf16[64,256]{1,0:T(8,128)(2,1)}) custom-call(bf16[4,8192]{1,0:T(4,128)(2,1)} %q_ref.1, bf16[4,512,128]{2,1,0:T(8,128)(2,1)} %bitcast.8, bf16[4,512,128]{2,1,0:T(8,128)(2,1)} %bitcast.9, s32[4]{0:T(128)} %len_ref.1, bf16[64,256]{1,0:T(8,128)(2,1)} %res_ref.1, bf16[256,4096]{1,0:T(8,128)(2,1)} %wo_hbm.1, ...), custom_call_target="tpu_custom_call" | custom-call | tf_op jit(solution)/shard_map/layer/pallas_call | solution.py:464
  78.1 1.4 %copy.18 = bf16[64,256]{1,0:T(8,128)(2,1)} copy(bf16[64,256]{1,0:T(8,128)(2,1)} %get-tuple-element.4) | data formatting | bytes 65536
  79.4 1.4 %copy.19 = bf16[64,256]{1,0:T(8,128)(2,1)} copy(bf16[64,256]{1,0:T(8,128)(2,1)} %get-tuple-element.5) | data formatting | bytes 65536

commit v3 on v2

--- a/solution.py
+++ b/solution.py
@@ -212,7 +212,8 @@
     hid_ref, mix_ref,
     k_v, v_v, wo_v, wg_v, wu_v, wd_v, local_sems,
     lay, qlay, sblk, ctx, part, part_in, hid_all, sq_all,
-    gate_acc, up_acc, act, own, tmp, core_in, xout, x_in, zout, up_in, down_in, yout, y_in,
+    gate_acc, up_acc, act, own, fin, tmp, core_in, y0_out, y0_in, x1_out, x1_in, x0_out, x0_in,
+    y1_out, y1_in, zout, up_in, down_in,
     c_send, c_recv, h_send, h_recv, p_send, p_recv, r_send, r_recv,
 ):
     f32, bf16 = jnp.float32, jnp.bfloat16
@@ -223,8 +224,8 @@
     barrier = pltpu.get_barrier_semaphore()
     pairs = [(k_hbm, k_v), (v_hbm, v_v), (wo_hbm, wo_v), (wg_hbm, wg_v), (wu_hbm, wu_v), (wd_hbm, wd_v)]
     loads = [pltpu.make_async_copy(s, d, local_sems.at[i]) for i, (s, d) in enumerate(pairs)]
-    for d in loads:
-        d.start()
+    loads[0].start()
+    loads[1].start()
     for dev in ((ec, y), (ex, y), (e, 1 - y)):
         pl.semaphore_signal(barrier, inc=1, device_id=dev, device_id_type=MESH)
 
@@ -241,6 +242,8 @@
         qlay[h * 8 : h * 8 + rows, :] = q_ref[:, h * 128 : (h + 1) * 128].astype(f32)
     loads[0].wait()
     loads[1].wait()
+    for d in loads[2:]:
+        d.start()
     col = lax.broadcasted_iota(jnp.int32, (64, 512), 1)
     head = lax.broadcasted_iota(jnp.int32, (64, 512), 0)
     same = (col % 4) == (head // 16)
@@ -338,106 +341,121 @@
 
     def block(zz, xx, cc):
         cols = pl.ds(pl.multiple_of((zz * 4 + xx * 2 + cc) * 256, 256), 256)
-        return jnp.dot(act[...], wd_v[:, cols], preferred_element_type=f32) * weight
+        p = jnp.dot(act[...], wd_v[:, cols], preferred_element_type=f32) * weight
+        return p.reshape(2, 2, 32, 256)
+
+    mirror = z // 2
+    near_z = z + mirror * (3 - 2 * z)
+
+    def far_first(i):
+        o = (3, 2, 1 - near_z, near_z)[i]
+        return o + mirror * (3 - 2 * o)
 
     def core_copy(b):
         return remote(tmp.at[b], core_in.at[b], r_send.at[b], r_recv.at[b], (ec, y))
 
-    def x_copy(b):
-        return remote(xout.at[b], x_in.at[b], r_send.at[8 + b], r_recv.at[8 + b], (ex, y))
-
-    def other_core(i, _):
-        xx = (1 - x + i // 4) % 2
-        b = xx * 4 + i % 4
-        tmp[b] = block(i % 4, xx, 1 - c).astype(bf16)
-        core_copy(b).start()
-        return 0
-
-    lax.fori_loop(0, 8, other_core, 0)
-
-    def far(zz, _):
-        p = block(zz, 1 - x, c)
-        b = (1 - x) * 4 + zz
-        core_copy(b).wait_recv()
-        xout[zz] = (p + core_in[b].astype(f32)).astype(bf16)
-        x_copy(zz).start()
-        return 0
-
-    lax.fori_loop(0, 4, far, 0)
-
-    def near(zz, _):
-        p = block(zz, x, c)
-        b = x * 4 + zz
-        core_copy(b).wait_recv()
-        own[zz] = p + core_in[b].astype(f32)
-        return 0
-
-    lax.fori_loop(0, 4, near, 0)
-
-    def x_done(zz, _):
-        x_copy(zz).wait_recv()
-        own[zz] = own[zz] + x_in[zz].astype(f32)
-        return 0
-
-    lax.fori_loop(0, 4, x_done, 0)
+    def y0_copy(b):
+        return remote(y0_out.at[b], y0_in.at[b], r_send.at[8 + b], r_recv.at[8 + b], (e, 1 - y))
+
+    def x1_copy(zz):
+        return remote(x1_out.at[zz], x1_in.at[zz], r_send.at[16 + zz], r_recv.at[16 + zz], (ex, y))
+
+    def x0_copy(zz):
+        return remote(x0_out.at[zz], x0_in.at[zz], r_send.at[20 + zz], r_recv.at[20 + zz], (ex, y))
+
+    def y1_copy(zz):
+        return remote(y1_out.at[zz], y1_in.at[zz], r_send.at[24 + zz], r_recv.at[24 + zz], (e, 1 - y))
 
     def up_copy(zz):
-        return remote(zout.at[zz], up_in.at[zz], r_send.at[12 + zz], r_recv.at[12 + zz], (e + 4, y))
+        return remote(zout.at[zz], up_in.at[zz], r_send.at[28 + zz], r_recv.at[28 + zz], (e + 4, y))
 
     def down_copy(zz):
-        return remote(zout.at[zz], down_in.at[zz], r_send.at[12 + zz], r_recv.at[16 + zz], (e - 4, y))
-
-    for k in range(NZ - 1, 0, -1):
-
-        @pl.when(z + k <= NZ - 1)
-        def _(k=k):
-            zz = z + k
-
-            @pl.when(z > 0)
+        return remote(zout.at[zz], down_in.at[zz], r_send.at[28 + zz], r_recv.at[32 + zz], (e - 4, y))
+
+    for i in range(NZ):
+        zz = far_first(i)
+        for xx in (1 - x, x):
+            b = xx * 4 + zz
+            tmp[b] = block(zz, xx, 1 - c).astype(bf16)
+            core_copy(b).start()
+
+    for i in range(NZ):
+        zz = far_first(i)
+        for n, xx in enumerate((1 - x, x)):
+            b = xx * 4 + zz
+            own[b] = block(zz, xx, c)
+            core_copy(b).wait_recv()
+            own[b] = own[b] + core_in[b].astype(f32)
+            y0_out[b] = own[b, 1 - y, 0].astype(bf16)
+            y0_copy(b).start()
+            if n == 0:
+                x1_out[zz] = own[b, :, 1].astype(bf16)
+                x1_copy(zz).start()
+
+    for i in range(NZ):
+        zz = far_first(i)
+        far, near = (1 - x) * 4 + zz, x * 4 + zz
+        x1_copy(zz).wait_recv()
+        y1_out[zz] = (own[near, 1 - y, 1] + x1_in[zz, 1 - y].astype(f32)).astype(bf16)
+        y1_copy(zz).start()
+        y0_copy(far).wait_recv()
+        x0_out[zz] = (own[far, y, 0] + y0_in[far].astype(f32)).astype(bf16)
+        x0_copy(zz).start()
+
+    for i in range(NZ):
+        zz = far_first(i)
+        near = x * 4 + zz
+        y0_copy(near).wait_recv()
+        x0_copy(zz).wait_recv()
+        y1_copy(zz).wait_recv()
+        fin[zz, 0] = own[near, y, 0] + y0_in[near].astype(f32) + x0_in[zz].astype(f32)
+        fin[zz, 1] = own[near, y, 1] + x1_in[zz, y].astype(f32) + y1_in[zz].astype(f32)
+
+        if i < NZ - 1:
+
+            @pl.when(zz > z)
             def _():
-                up_copy(zz).wait_recv()
-                own[zz] = own[zz] + up_in[zz].astype(f32)
-
-            zout[zz] = own[zz].astype(bf16)
-            up_copy(zz).start()
-
-        @pl.when(z - k >= 0)
-        def _(k=k):
-            zz = z - k
-
-            @pl.when(z < NZ - 1)
+                @pl.when(z > 0)
+                def _():
+                    up_copy(zz).wait_recv()
+                    fin[zz] = fin[zz] + up_in[zz].astype(f32)
+
+                zout[zz] = fin[zz].astype(bf16)
+                up_copy(zz).start()
+
+            @pl.when(zz < z)
             def _():
-                down_copy(zz).wait_recv()
-                own[zz] = own[zz] + down_in[zz].astype(f32)
-
-            zout[zz] = own[zz].astype(bf16)
-            down_copy(zz).start()
+                @pl.when(z < NZ - 1)
+                def _():
+                    down_copy(zz).wait_recv()
+                    fin[zz] = fin[zz] + down_in[zz].astype(f32)
+
+                zout[zz] = fin[zz].astype(bf16)
+                down_copy(zz).start()
 
     @pl.when(z > 0)
     def _():
         up_copy(z).wait_recv()
-        own[z] = own[z] + up_in[z].astype(f32)
+        fin[z] = fin[z] + up_in[z].astype(f32)
 
     @pl.when(z < NZ - 1)
     def _():
         down_copy(z).wait_recv()
-        own[z] = own[z] + down_in[z].astype(f32)
-
-    final = own.at[z].reshape(2, 64, 256)
-    yout[...] = final[1 - y].astype(bf16)
-    ysend = remote(yout, y_in, p_send.at[4], p_recv.at[4], (e, 1 - y))
-    ysend.start()
-    ysend.wait_recv()
-    mix_ref[...] = (final[y] + y_in[...].astype(f32)).astype(bf16)
-
-    for d in (swap, psend, hs, qs, ysend):
+        fin[z] = fin[z] + down_in[z].astype(f32)
+
+    mix_ref[...] = fin[z].reshape(64, 256).astype(bf16)
+
+    for d in (swap, psend, hs, qs):
         d.wait_send()
     g1.wait_sends()
     g2.wait_sends()
     for b in range(8):
         core_copy(b).wait_send()
-    for b in range(4):
-        x_copy(b).wait_send()
+        y0_copy(b).wait_send()
+    for zz in range(NZ):
+        x1_copy(zz).wait_send()
+        x0_copy(zz).wait_send()
+        y1_copy(zz).wait_send()
     for k in range(1, NZ):
 
         @pl.when(z + k <= NZ - 1)
@@ -473,10 +491,14 @@
             V((256, 128), f32), V((512, 128), f32), V((2, 16, 1024), bf16), V((16, 2, 16, 1024), bf16),
             V((2, 64, 256), f32), V((64, 256), f32), V((16, 2, 64, 256), bf16), V((16, 2, 8, 128), f32),
             V((3, 128, 256), f32), V((3, 128, 256), f32), V((128, 768), bf16),
-            V((4, 128, 256), f32), V((8, 128, 256), bf16), V((8, 128, 256), bf16),
-            V((4, 128, 256), bf16), V((4, 128, 256), bf16), V((4, 128, 256), bf16),
-            V((4, 128, 256), bf16), V((4, 128, 256), bf16), V((64, 256), bf16), V((64, 256), bf16),
-            S((1, 18)), S((1, 18)), S((2, 18)), S((2, 18)), S((5,)), S((5,)), S((20,)), S((20,)),
+            V((8, 2, 2, 32, 256), f32), V((4, 2, 32, 256), f32),
+            V((8, 2, 2, 32, 256), bf16), V((8, 2, 2, 32, 256), bf16),
+            V((8, 32, 256), bf16), V((8, 32, 256), bf16),
+            V((4, 2, 32, 256), bf16), V((4, 2, 32, 256), bf16),
+            V((4, 32, 256), bf16), V((4, 32, 256), bf16),
+            V((4, 32, 256), bf16), V((4, 32, 256), bf16),
+            V((4, 2, 32, 256), bf16), V((4, 2, 32, 256), bf16), V((4, 2, 32, 256), bf16),
+            S((1, 18)), S((1, 18)), S((2, 18)), S((2, 18)), S((4,)), S((4,)), S((36,)), S((36,)),
         ],
         compiler_params=pltpu.CompilerParams(
             collective_id=0, has_side_effects=True, vmem_limit_bytes=62 * 1024 * 1024

time: 81.2 us -> 76.4 us (0.941)
  Pallas kernels: 73.4 us -> 68.6 us
    pallas_call x1, Pallas kernels: 73.4 us -> 68.6 us  [fused_body(): pl.pallas_call(layer_kernel, name='layer', out_shape=(jax.ShapeDtypeStruc...]
where the time goes in v3:
time: 76.4 us; the launch traced here: 76.1 us
  Pallas kernels  68.6 us (90%)
  local copies, waits for them, and re-layouts  6.77 us (9%)
    pallas_call x1, Pallas kernels, fused_body(): pl.pallas_call(layer_kernel, name='layer', out_shape=(jax.ShapeDtypeStruc...  68.6 us
    unnamed x4, local copies, waits for them, and re-layouts  5.55 us

profile of v3, /device:TPU:0, one launch (start us, length us, event | category | flops | bytes accessed | tf_op | source)
XLA Modules:
  0.0 76.1 jit_solution(10041563880024149308)
XLA Ops:
  0.6 1.2 %reshape.15.gain_ref = bf16[1,256]{1,0:T(2,128)(2,1)} reshape(bf16[256]{0:T(256)(128)(2,1)} %param.18) | data formatting | bytes 1024 | tf_op jit(solution)/shard_map/reshape | solution.py:507
  1.8 1.4 %copy.15.gates_ref = bf16[128,8]{1,0:T(8,128)(2,1)} copy(bf16[128,8]{0,1:T(8,128)(2,1)} %param.20) | data formatting | bytes 4096 | tf_op args[8]
  3.2 1.4 %copy.14.ids_ref = s32[128,8]{1,0:T(8,128)} copy(s32[128,8]{0,1:T(8,128)} %param.19) | data formatting | bytes 8192 | tf_op args[7]
  4.7 68.6 %layer.1 = (bf16[64,256]{1,0:T(8,128)(2,1)}, bf16[64,256]{1,0:T(8,128)(2,1)}) custom-call(bf16[4,8192]{1,0:T(4,128)(2,1)} %q_ref.1, bf16[4,512,128]{2,1,0:T(8,128)(2,1)} %bitcast.8, bf16[4,512,128]{2,1,0:T(8,128)(2,1)} %bitcast.9, s32[4]{0:T(128)} %len_ref.1, bf16[64,256]{1,0:T(8,128)(2,1)} %res_ref.1, bf16[256,4096]{1,0:T(8,128)(2,1)} %wo_hbm.1, ...), custom_call_target="tpu_custom_call" | custom-call | tf_op jit(solution)/shard_map/layer/pallas_call | solution.py:482
  73.3 1.4 %copy.18 = bf16[64,256]{1,0:T(8,128)(2,1)} copy(bf16[64,256]{1,0:T(8,128)(2,1)} %get-tuple-element.4) | data formatting | bytes 65536
  74.7 1.4 %copy.19 = bf16[64,256]{1,0:T(8,128)(2,1)} copy(bf16[64,256]{1,0:T(8,128)(2,1)} %get-tuple-element.5) | data formatting | bytes 65536

commit v4 on v3

--- a/solution.py
+++ b/solution.py
@@ -209,7 +209,7 @@
 def layer_kernel(
     q_ref, k_hbm, v_hbm, len_ref, res_ref, wo_hbm, gain_ref, ids_ref, gates_ref,
     wg_hbm, wu_hbm, wd_hbm,
-    hid_ref, mix_ref,
+    out_ref,
     k_v, v_v, wo_v, wg_v, wu_v, wd_v, local_sems,
     lay, qlay, sblk, ctx, part, part_in, hid_all, sq_all,
     gate_acc, up_acc, act, own, fin, tmp, core_in, y0_out, y0_in, x1_out, x1_in, x0_out, x0_in,
@@ -291,8 +291,8 @@
     psend.start()
     psend.wait_recv()
     hidden = res_ref[...].astype(f32) + (part[y] + part_in[...])
-    hid_ref[...] = hidden.astype(bf16)
-    hid_all[e, y] = (hidden * gain_ref[...].astype(f32)).astype(bf16)
+    out_ref[0] = hidden
+    hid_all[e, y] = (hidden * gain_ref[...].astype(f32).reshape(1, 256)).astype(bf16)
     ss = jnp.sum(hidden * hidden, axis=1, keepdims=True)
     place = lax.broadcasted_iota(jnp.int32, (64, 128), 0) + 64 * y
     lane = lax.broadcasted_iota(jnp.int32, (64, 128), 1)
@@ -331,8 +331,9 @@
     eye = lax.broadcasted_iota(jnp.int32, (128, 128), 0) == lax.broadcasted_iota(jnp.int32, (128, 128), 1)
     scale = jnp.sum(jnp.where(eye, scale_row, 0.0), axis=1, keepdims=True)
     gw = gates_ref[...].astype(f32)
-    gw = gw / jnp.sum(gw, axis=1, keepdims=True)
-    weight = jnp.sum(jnp.where(ids_ref[...] == e, gw, 0.0), axis=1, keepdims=True)
+    gw = gw / jnp.sum(gw, axis=0, keepdims=True)
+    weight_row = jnp.sum(jnp.where(ids_ref[...] == e, gw, 0.0), axis=0, keepdims=True)
+    weight = jnp.sum(jnp.where(eye, weight_row, 0.0), axis=1, keepdims=True)
     for n in range(3):
         g = gate_acc[n] * scale
         u = up_acc[n] * scale
@@ -443,7 +444,7 @@
         down_copy(z).wait_recv()
         fin[z] = fin[z] + down_in[z].astype(f32)
 
-    mix_ref[...] = fin[z].reshape(64, 256).astype(bf16)
+    out_ref[1] = fin[z].reshape(64, 256)
 
     for d in (swap, psend, hs, qs):
         d.wait_send()
@@ -479,12 +480,12 @@
     hb = pl.BlockSpec(memory_space=pl.ANY)
     sm = pl.BlockSpec(memory_space=pltpu.SMEM)
     V, S = pltpu.VMEM, pltpu.SemaphoreType.DMA
-    return pl.pallas_call(
+    out = pl.pallas_call(
         layer_kernel,
         name="layer",
-        out_shape=(jax.ShapeDtypeStruct((64, 256), bf16), jax.ShapeDtypeStruct((64, 256), bf16)),
+        out_shape=jax.ShapeDtypeStruct((2, 64, 256), f32),
         in_specs=[vm, hb, hb, sm, vm, hb, vm, vm, vm, hb, hb, hb],
-        out_specs=(vm, vm),
+        out_specs=vm,
         scratch_shapes=[
             V((rows, 512, 128), bf16), V((rows, 512, 128), bf16), V((256, 4096), bf16),
             V((768, 4096), bf16), V((768, 4096), bf16), V((768, 4096), bf16), S((6,)),
@@ -504,9 +505,10 @@
             collective_id=0, has_side_effects=True, vmem_limit_bytes=62 * 1024 * 1024
         ),
     )(
-        query, keys, values, lengths, residual, out_proj, norm_gain.reshape(1, -1), expert_ids,
-        gate_scores, w_gate[0], w_up[0], w_down[0],
-    )
+        query, keys, values, lengths, residual, out_proj, norm_gain, expert_ids.T,
+        gate_scores.T, w_gate[0], w_up[0], w_down[0],
+    )
+    return (out[0].astype(bf16), out[1].astype(bf16))
 
 
 def solution(mesh):

time: 76.4 us -> 71.1 us (0.931)
  local copies, waits for them, and re-layouts: 6.77 us -> 0.63 us
  other arithmetic: 0 us -> 0.91 us
    unnamed x4 -> x0, local copies, waits for them, and re-layouts: 5.55 us -> none
    reshape x1 -> x0, local copies, waits for them, and re-layouts: 1.22 us -> none  [fused_body(): norm_gain.reshape(1, -1)]
    another operation x0 -> x1, other arithmetic: none -> 0.91 us
where the time goes in v4:
time: 71.1 us; the launch traced here: 70.9 us
  Pallas kernels  68.7 us (97%)
  other arithmetic  0.91 us (1%)
    pallas_call x1, Pallas kernels, fused_body(): pl.pallas_call(layer_kernel, name='layer', out_shape=jax.ShapeDtypeStruct...  68.7 us

profile of v4, /device:TPU:0, one launch (start us, length us, event | category | flops | bytes accessed | tf_op | source)
XLA Modules:
  0.0 70.9 jit_solution(6248847224563108057)
XLA Ops:
  0.6 68.7 %layer.1 = f32[2,64,256]{2,1,0:T(8,128)} custom-call(bf16[4,8192]{1,0:T(4,128)(2,1)} %q_ref.1, bf16[4,512,128]{2,1,0:T(8,128)(2,1)} %bitcast.14, bf16[4,512,128]{2,1,0:T(8,128)(2,1)} %bitcast.15, s32[4]{0:T(128)} %len_ref.1, bf16[64,256]{1,0:T(8,128)(2,1)} %res_ref.1, bf16[256,4096]{1,0:T(8,128)(2,1)} %wo_hbm.1, bf16[256]{0:T(256)(128)(2,1)} %gain_ref.1, ...), custom_call_target="tpu_custom_call" | custom-call | tf_op jit(solution)/shard_map/layer/pallas_call | solution.py:483
  69.3 0.9 %convert.4 = bf16[2,64,256]{2,1,0:T(8,128)(2,1)S(1)} convert(f32[2,64,256]{2,1,0:T(8,128)} %layer.1) | non-fusion elementwise | flops 32768 | bytes 196608 | tf_op jit(solution)/shard_map/convert.1
  70.2 0.6 slice_bitcast_fusion
